TPU v7x, 32 devices: a whole 2x2x4 slice. The times are simulated.
32 devices in a mesh: groups: 2 (over y), rows: 4 (over z), cols: 2 (over x), sub: 2 (over core).
Axes of the slice: x: 2, y: 2, z: 4, core: 2. Of those that a mesh axis runs over, the one named last changes fastest.
Arguments:
- data_rows: bfloat16 [16384, 256], P(('groups', 'rows')), parts along dimension 0, may hold values from -6 to 6
- landmarks: bfloat16 [4096, 256], P(('groups', 'rows', 'cols')), parts along dimension 0, may hold values from -6 to 6
- factor: bfloat16 [4096, 2048], P(('groups', 'rows', 'cols'), 'sub'), parts along dimension 0, may hold values from -0.02734375 to 0.02734375
- chosen_owner: int32 [2048, 1], P('groups'), parts along dimension 0, may hold values from 0 to 3; in each aligned block of 256 rows (0 to 255, 256 to 511, ...) at most 256 rows name the same one
- chosen_local: int32 [2048], P('groups'), parts along dimension 0, may hold values from 0 to 2047
Outputs:
- leverage: float32 [16384], P(('groups', 'rows', 'cols')), parts along dimension 0
- panel: float32 [2048, 256], P(('groups', 'rows'), 'cols'), parts along dimension 0
There are 2 independent parts, one for each index of `groups`. A program takes and returns all parts, laid end to end along the dimension named above; each array names one. Nothing has to cross between parts.
Inputs may be any that keep to these rules, and one draw needn't show every extreme that they name: `chosen_owner`: in each aligned block of 256 chosen rows no owner appears more than 256 times, and in some block one owner appears exactly 256 times.
All inputs are finite; a program needn't handle non-finite values.
Results may differ from a plain program's by a relative error of at most 0.00039.
Values may be sent and summed in bfloat16 or wider, within the bound.
A program may use at most 64 MiB of HBM per device.

v0:
```python
import math
import jax
import jax.numpy as jnp
from jax import lax
from jax.sharding import PartitionSpec as P

PANEL_DEV = 64


def squared_norms(rows_in):
    return jnp.sum(jnp.square(rows_in.astype(jnp.float32)), axis=1)


def kernel_values(left, right, right_sq, rate_value, depth):
    left_sq = squared_norms(left)
    cross = lax.dot_general(
        left, right, (((1,), (1,)), ((), ())), preferred_element_type=jnp.float32
    )
    distance = left_sq[:, None] + right_sq[None, :] - 2.0 * cross
    return jnp.exp(rate_value * (2.0 * depth - distance))


def shards(data_rows, landmarks, factor, chosen_owner, chosen_local):
    slab_rows, depth = data_rows.shape
    rate_value = 0.3 / math.sqrt(8.0 * depth)
    amplitude = math.exp(2.0 * rate_value * depth)
    col_count = lax.axis_size("cols")
    sub_count = lax.axis_size("sub")
    row_count = lax.axis_size("rows")
    col_index = lax.axis_index("cols")
    sub_index = lax.axis_index("sub")
    row_index = lax.axis_index("rows")
    every_land = lax.all_gather(landmarks, ("rows", "cols"), axis=0, tiled=True)
    mixed = lax.all_to_all(factor, "cols", split_axis=1, concat_axis=0, tiled=True)
    factor_cols = lax.all_gather(mixed, "rows", axis=0, tiled=True)
    land_sq = squared_norms(every_land)
    block_rows = math.gcd(slab_rows, 256)
    blocks = data_rows.reshape(-1, block_rows, depth)

    def block_total(block):
        values = kernel_values(block, every_land, land_sq, rate_value, depth).astype(jnp.bfloat16)
        projected = jnp.dot(values, factor_cols, preferred_element_type=jnp.float32)
        return jnp.sum(projected * projected, axis=1)

    totals = lax.map(block_total, blocks).reshape(-1)
    row_totals = lax.psum_scatter(totals, "cols", scatter_dimension=0, tiled=True)
    approx = lax.psum(row_totals, "sub")
    leverage = (amplitude - approx) / 8.0
    block_owners = chosen_owner[:, 0].reshape(row_count, -1)
    local_rows = chosen_local.reshape(row_count, -1)
    chosen_dev = block_owners.shape[1]
    capacity = 8 * max(1, chosen_dev // (2 * row_count))
    mine_mask = (block_owners == row_index).astype(jnp.int32)
    slot_rank = jnp.cumsum(mine_mask, axis=1) - mine_mask
    replicas = col_count * sub_count
    share_size = capacity // replicas
    replica_index = col_index * sub_count + sub_index
    slot_ids = replica_index * share_size + jnp.arange(share_size, dtype=jnp.int32)
    picked = (mine_mask[:, None, :] == 1) & (slot_rank[:, None, :] == slot_ids[None, :, None])
    source = jnp.sum(jnp.where(picked, local_rows[:, None, :], 0), axis=2)
    filled = jnp.any(picked, axis=2)
    picked_rows = jnp.take(data_rows, source.reshape(-1), axis=0).reshape(
        row_count, share_size, depth
    )
    outgoing = jnp.where(filled[:, :, None], picked_rows, jnp.zeros((), jnp.bfloat16))
    moved = lax.all_to_all(outgoing, "rows", split_axis=0, concat_axis=0, tiled=True)
    arrived = lax.all_gather(moved, ("cols", "sub"), axis=1, tiled=True)
    block_owner = lax.dynamic_index_in_dim(block_owners, row_index, 0, keepdims=False)
    before = jnp.tril(jnp.ones((chosen_dev, chosen_dev), jnp.bool_), -1)
    matched = (block_owner[:, None] == block_owner[None, :]) & before
    own_rank = jnp.sum(matched.astype(jnp.int32), axis=1)
    flattened = arrived.reshape(row_count * capacity, depth)
    chosen_rows = jnp.take(flattened, block_owner * capacity + own_rank, axis=0)
    per_block = PANEL_DEV // col_count
    piece = lax.dynamic_slice_in_dim(chosen_rows, col_index * per_block, per_block, 0)
    column_rows = lax.all_gather(piece, "rows", axis=0, tiled=True)
    panel = kernel_values(chosen_rows, column_rows, squared_norms(column_rows), rate_value, depth)
    return (leverage, panel)


def solution(mesh):
    placed = (
        P(("groups", "rows"), None),
        P(("groups", "rows", "cols"), None),
        P(("groups", "rows", "cols"), "sub"),
        P("groups", None),
        P("groups"),
    )
    return jax.shard_map(
        shards,
        mesh=mesh,
        in_specs=placed,
        out_specs=(P(("groups", "rows", "cols")), P(("groups", "rows"), "cols")),
        check_vma=False,
    )
```

profile of v0, /device:TPU:0, one launch (start us, length us, event | category | flops | bytes accessed | tf_op | source)
XLA Modules:
  0.0 143.4 jit_solution(4056909570043862323)
XLA Ops:
  7.9 1.9 %copy.21 = bf16[32,2,8,512]{3,2,0,1:T(8,128)(2,1)} copy(bf16[32,2,8,512]{3,2,1,0:T(8,128)(2,1)} %bitcast.51) | data formatting | bytes 1048576 | tf_op jit(solution)/shard_map/all_to_all | solution.py:34
  9.8 4.2 %all-to-all-start = ((bf16[256,2,512]{2,0,1:T(8,128)(2,1)}), bf16[256,2,512]{2,0,1:T(8,128)(2,1)S(1)}, u32[]{:S(2)}, u32[]{:S(2)}) async-start(bf16[256,2,512]{2,0,1:T(8,128)(2,1)} %bitcast.37), calls=%async_computation | async-start | bytes 1048576 | tf_op jit(solution)/shard_map/all_to_all | solution.py:34
  15.3 1.2 reduce-window.6
  16.9 5.9 %all-to-all-done = bf16[256,2,512]{2,0,1:T(8,128)(2,1)S(1)} async-done(((bf16[256,2,512]{2,0,1:T(8,128)(2,1)}), bf16[256,2,512]{2,0,1:T(8,128)(2,1)S(1)}, u32[]{:S(2)}, u32[]{:S(2)}) %all-to-all-start) | async-done | bytes 524320 | tf_op jit(solution)/shard_map/all_to_all | solution.py:34
  24.0 1.2 gather_fusion
  26.2 5.1 %all-to-all-start.1 = ((bf16[4,64,256]{2,1,0:T(8,128)(2,1)}), bf16[4,64,256]{2,1,0:T(8,128)(2,1)S(1)}, u32[]{:S(2)}, u32[]{:S(2)}) async-start(bf16[4,64,256]{2,1,0:T(8,128)(2,1)} %select_select_fusion), calls=%async_computation.1 | async-start | bytes 262144 | tf_op jit(solution)/shard_map/all_to_all | solution.py:66
  32.7 4.5 %all-to-all-done.1 = bf16[4,64,256]{2,1,0:T(8,128)(2,1)S(1)} async-done(((bf16[4,64,256]{2,1,0:T(8,128)(2,1)}), bf16[4,64,256]{2,1,0:T(8,128)(2,1)S(1)}, u32[]{:S(2)}, u32[]{:S(2)}) %all-to-all-start.1) | async-done | bytes 131104 | tf_op jit(solution)/shard_map/all_to_all | solution.py:66
  37.2 9.6 %all_gather.14 = bf16[4,256,256]{2,1,0:T(8,128)(2,1)S(1)} all-gather(bf16[4,64,256]{2,1,0:T(8,128)(2,1)S(1)} %all-to-all-done.1), channel_id=1, replica_groups=mesh['groups'=2,'rows'=4,'cols'=2,'sub'=2] {'cols','sub'}, dimensions={1}, use_global_device_ids=true | all-gather | bytes 655360 | tf_op jit(solution)/shard_map/all_gather | solution.py:67
  46.8 1.1 gather_fusion.1
  48.2 13.2 %all_gather.15 = bf16[128,256]{1,0:T(8,128)(2,1)S(1)} all-gather(bf16[32,256]{1,0:T(8,128)(2,1)S(1)} %constant_dynamic-slice_fusion), channel_id=1, replica_groups=mesh['groups'=2,'rows'=4,'cols'=2,'sub'=2] {'rows'}, dimensions={0}, use_global_device_ids=true | all-gather | bytes 81920 | tf_op jit(solution)/shard_map/all_gather | solution.py:76
  61.5 0.9 fusion.18
  62.4 1.6 %multiply_reduce_fusion.1 = f32[2048]{0:T(1024)S(1)} fusion(bf16[2048,256]{1,0:T(8,128)(2,1)} %all-gather.3.cloned.1.call-done), kind=kLoop, calls=%fused_computation.17 | loop fusion | flops 1570816 | bytes 1056768 | tf_op jit(solution)/shard_map/reduce_sum | solution.py:11
  64.0 36.9 %all-gather.5.cloned.1.call-done = bf16[2048,512]{1,0:T(8,128)(2,1)} async-done(((bf16[512,512]{1,0:T(8,128)(2,1)}), bf16[2048,512]{1,0:T(8,128)(2,1)}) %all-gather.5.cloned.1.call-update) | async-done | bytes 2097168 | tf_op jit(solution)/shard_map/all_gather | solution.py:35
  100.9 27.6 %while.10 = (s32[]{:T(128)}, f32[8,256]{1,0:T(8,128)S(1)}, bf16[8,256,256]{2,1,0:T(8,128)(2,1)S(1)}, f32[2048]{0:T(1024)S(1)}, bf16[2048,256]{1,0:T(8,128)(2,1)}...) while((s32[]{:T(128)}, f32[8,256]{1,0:T(8,128)S(1)}, bf16[8,256,256]{2,1,0:T(8,128)(2,1)S(1)}, ...), condition=%wide.region_4.5_spmd, body=%wide.region_1.4_spmd.sunk | while | flops 808910336 | bytes 3421289 | solution.py:45
  101.0 3.3 %fusion.32 = f32[256]{0:T(256)S(1)} fusion(bf16[2048,512]{1,0:T(8,128)(2,1)} %get-tuple-element.109, bf16[2048,256]{1,0:T(8,128)(2,1)} %get-tuple-element.108, f32[2048]{0:T(1024)S(1)} %get-tuple-element.107, f32[256]{0:T(256)S(1)} %multiply_reduce_fusion.5, bf16[8,256,256]{2,1,0:T(8,128)(2,1)S(1)} %get-tuple-element.106, s32[]{:T(128)S(6)} %copy.25), kind=kOutput, calls=%fused_computation.9.clone.1 | convolution fusion | flops 808713984 | bytes 3287044 | tf_op jit(solution)/shard_map/while/body/eval_jaxpr/dot_general | solution.py:42
  104.5 3.3 %fusion.32 = f32[256]{0:T(256)S(1)} fusion(bf16[2048,512]{1,0:T(8,128)(2,1)} %get-tuple-element.109, bf16[2048,256]{1,0:T(8,128)(2,1)} %get-tuple-element.108, f32[2048]{0:T(1024)S(1)} %get-tuple-element.107, f32[256]{0:T(256)S(1)} %multiply_reduce_fusion.5, bf16[8,256,256]{2,1,0:T(8,128)(2,1)S(1)} %get-tuple-element.106, s32[]{:T(128)S(6)} %copy.25), kind=kOutput, calls=%fused_computation.9.clone.1 | convolution fusion | flops 808713984 | bytes 3287044 | tf_op jit(solution)/shard_map/while/body/eval_jaxpr/dot_general | solution.py:42
  107.9 3.3 %fusion.32 = f32[256]{0:T(256)S(1)} fusion(bf16[2048,512]{1,0:T(8,128)(2,1)} %get-tuple-element.109, bf16[2048,256]{1,0:T(8,128)(2,1)} %get-tuple-element.108, f32[2048]{0:T(1024)S(1)} %get-tuple-element.107, f32[256]{0:T(256)S(1)} %multiply_reduce_fusion.5, bf16[8,256,256]{2,1,0:T(8,128)(2,1)S(1)} %get-tuple-element.106, s32[]{:T(128)S(6)} %copy.25), kind=kOutput, calls=%fused_computation.9.clone.1 | convolution fusion | flops 808713984 | bytes 3287044 | tf_op jit(solution)/shard_map/while/body/eval_jaxpr/dot_general | solution.py:42
  111.4 3.3 %fusion.32 = f32[256]{0:T(256)S(1)} fusion(bf16[2048,512]{1,0:T(8,128)(2,1)} %get-tuple-element.109, bf16[2048,256]{1,0:T(8,128)(2,1)} %get-tuple-element.108, f32[2048]{0:T(1024)S(1)} %get-tuple-element.107, f32[256]{0:T(256)S(1)} %multiply_reduce_fusion.5, bf16[8,256,256]{2,1,0:T(8,128)(2,1)S(1)} %get-tuple-element.106, s32[]{:T(128)S(6)} %copy.25), kind=kOutput, calls=%fused_computation.9.clone.1 | convolution fusion | flops 808713984 | bytes 3287044 | tf_op jit(solution)/shard_map/while/body/eval_jaxpr/dot_general | solution.py:42
  114.8 3.3 %fusion.32 = f32[256]{0:T(256)S(1)} fusion(bf16[2048,512]{1,0:T(8,128)(2,1)} %get-tuple-element.109, bf16[2048,256]{1,0:T(8,128)(2,1)} %get-tuple-element.108, f32[2048]{0:T(1024)S(1)} %get-tuple-element.107, f32[256]{0:T(256)S(1)} %multiply_reduce_fusion.5, bf16[8,256,256]{2,1,0:T(8,128)(2,1)S(1)} %get-tuple-element.106, s32[]{:T(128)S(6)} %copy.25), kind=kOutput, calls=%fused_computation.9.clone.1 | convolution fusion | flops 808713984 | bytes 3287044 | tf_op jit(solution)/shard_map/while/body/eval_jaxpr/dot_general | solution.py:42
  118.3 3.3 %fusion.32 = f32[256]{0:T(256)S(1)} fusion(bf16[2048,512]{1,0:T(8,128)(2,1)} %get-tuple-element.109, bf16[2048,256]{1,0:T(8,128)(2,1)} %get-tuple-element.108, f32[2048]{0:T(1024)S(1)} %get-tuple-element.107, f32[256]{0:T(256)S(1)} %multiply_reduce_fusion.5, bf16[8,256,256]{2,1,0:T(8,128)(2,1)S(1)} %get-tuple-element.106, s32[]{:T(128)S(6)} %copy.25), kind=kOutput, calls=%fused_computation.9.clone.1 | convolution fusion | flops 808713984 | bytes 3287044 | tf_op jit(solution)/shard_map/while/body/eval_jaxpr/dot_general | solution.py:42
  121.7 3.3 %fusion.32 = f32[256]{0:T(256)S(1)} fusion(bf16[2048,512]{1,0:T(8,128)(2,1)} %get-tuple-element.109, bf16[2048,256]{1,0:T(8,128)(2,1)} %get-tuple-element.108, f32[2048]{0:T(1024)S(1)} %get-tuple-element.107, f32[256]{0:T(256)S(1)} %multiply_reduce_fusion.5, bf16[8,256,256]{2,1,0:T(8,128)(2,1)S(1)} %get-tuple-element.106, s32[]{:T(128)S(6)} %copy.25), kind=kOutput, calls=%fused_computation.9.clone.1 | convolution fusion | flops 808713984 | bytes 3287044 | tf_op jit(solution)/shard_map/while/body/eval_jaxpr/dot_general | solution.py:42
  125.2 3.3 %fusion.32 = f32[256]{0:T(256)S(1)} fusion(bf16[2048,512]{1,0:T(8,128)(2,1)} %get-tuple-element.109, bf16[2048,256]{1,0:T(8,128)(2,1)} %get-tuple-element.108, f32[2048]{0:T(1024)S(1)} %get-tuple-element.107, f32[256]{0:T(256)S(1)} %multiply_reduce_fusion.5, bf16[8,256,256]{2,1,0:T(8,128)(2,1)S(1)} %get-tuple-element.106, s32[]{:T(128)S(6)} %copy.25), kind=kOutput, calls=%fused_computation.9.clone.1 | convolution fusion | flops 808713984 | bytes 3287044 | tf_op jit(solution)/shard_map/while/body/eval_jaxpr/dot_general | solution.py:42
  128.5 5.0 %all-reduce = f32[2048]{0:T(1024)S(1)} all-reduce(f32[2048]{0:T(1024)S(1)} %bitcast.53), channel_id=2, replica_groups=mesh['groups'=2,'rows'=4,'cols'=2,'sub'=2] {'cols'}, use_global_device_ids=true, to_apply=%region_5.6.clone | all-reduce | flops 2048 | bytes 16384
  133.5 2.5 %psum.7 = f32[1024]{0:T(1024)S(1)} all-reduce(f32[1024]{0:T(1024)S(1)} %dynamic-slice.1), channel_id=1, replica_groups=mesh['groups'=2,'rows'=4,'cols'=2,'sub'=2] {'sub'}, use_global_device_ids=true, to_apply=%region_6.7 | all-reduce | flops 1024 | bytes 8192 | tf_op jit(solution)/shard_map/psum | solution.py:47
  (66 shorter events, 7.5 us)
Async XLA Ops:
  7.2 7.4 %copy-start.2 = (s32[1024,1]{0,1:T(1,128)S(1)}, s32[1024,1]{0,1:T(1,128)}, u32[]{:S(2)}) copy-start(s32[1024,1]{0,1:T(1,128)} %param.10) | copy-start | bytes 12292
  7.2 16.4 %copy-start.3 = (s32[1024]{0:T(1024)S(1)}, s32[1024]{0:T(1024)}, u32[]{:S(2)}) copy-start(s32[1024]{0:T(1024)} %param.11) | copy-start | bytes 12292
  7.2 16.8 %copy-start = (bf16[2048,256]{1,0:T(8,128)(2,1)S(1)}, bf16[2048,256]{1,0:T(8,128)(2,1)}, u32[]{:S(2)}) copy-start(bf16[2048,256]{1,0:T(8,128)(2,1)} %param.7) | copy-start | bytes 3145732
  7.2 55.2 %all-gather.3.cloned.1.call-start = ((), (), s32[]{:S(2)}) async-start(), calls=%async_computation.2 | async-start | bytes 1179648 | tf_op jit(solution)/shard_map/all_gather | solution.py:33
  7.9 23.4 %copy-start.4 = (u32[32]{0:T(128)S(1)}, u32[32]{0:T(128)}, u32[]{:S(2)}) copy-start(u32[32]{0:T(128)} %constant.104) | copy-start | bytes 388
  9.8 13.0 %all-to-all-start = ((bf16[256,2,512]{2,0,1:T(8,128)(2,1)}), bf16[256,2,512]{2,0,1:T(8,128)(2,1)S(1)}, u32[]{:S(2)}, u32[]{:S(2)}) async-start(bf16[256,2,512]{2,0,1:T(8,128)(2,1)} %bitcast.37), calls=%async_computation | async-start | bytes 1048576 | tf_op jit(solution)/shard_map/all_to_all | solution.py:34
  14.0 86.8 %all-gather.5.cloned.1.call-start = ((), (), s32[]{:S(2)}) async-start(), calls=%async_computation.3 | async-start | bytes 2621440 | tf_op jit(solution)/shard_map/all_gather | solution.py:35
  22.8 0.8 copy-start.1
  26.2 11.0 %all-to-all-start.1 = ((bf16[4,64,256]{2,1,0:T(8,128)(2,1)}), bf16[4,64,256]{2,1,0:T(8,128)(2,1)S(1)}, u32[]{:S(2)}, u32[]{:S(2)}) async-start(bf16[4,64,256]{2,1,0:T(8,128)(2,1)} %select_select_fusion), calls=%async_computation.1 | async-start | bytes 262144 | tf_op jit(solution)/shard_map/all_to_all | solution.py:66
Sparse Core Ops, SparseCore 0:
  10.1 44.1 all-gather.2
  55.9 44.9 all-gather.4
where the time goes:
time: 144 us; the launch traced here: 143 us
  waiting for transfers between devices  47.9 us (33%)
  blocking collectives  30.3 us (21%)
  matrix products  27 us (19%)
  between operations  14.8 us (10%)
  starting transfers between devices  9.39 us (7%)
  other arithmetic  6.97 us (5%)
  local copies, waits for them, and re-layouts  6.81 us (5%)
    all_gather x1, waiting for transfers between devices, shards(): factor_cols = lax.all_gather(mixed, 'rows', axis=0, tiled=True)  36.9 us
    dot_general x8, matrix products, block_total(): projected = jnp.dot(values, factor_cols, preferred_element_type=jnp.float32)  26.1 us
    all_gather x1, blocking collectives, shards(): column_rows = lax.all_gather(piece, 'rows', axis=0, tiled=True)  13.2 us
    all_gather x1, blocking collectives, shards(): arrived = lax.all_gather(moved, ('cols', 'sub'), axis=1, tiled=True)  9.63 us
    all_to_all x1, waiting for transfers between devices, shards(): lax.all_to_all(factor, 'cols', split_axis=1, concat_axis=0, tiled=True)  5.88 us
    all_to_all x1, starting transfers between devices, shards(): lax.all_to_all(outgoing, 'rows', split_axis=0, concat_axis=0, tiled=True)  5.12 us
    unnamed x1, blocking collectives  5 us
    all_to_all x1, waiting for transfers between devices, shards(): lax.all_to_all(outgoing, 'rows', split_axis=0, concat_axis=0, tiled=True)  4.48 us
  transfers between devices with their start and end apart: 4, of which 3 were waited for; matrix products, arithmetic and copies ran while one was open for 8% of the time, Pallas kernels for 0%

commit v1 on v0

--- a/solution.py
+++ b/solution.py
@@ -5,6 +5,17 @@
 from jax.sharding import PartitionSpec as P
 
 PANEL_DEV = 64
+
+
+def around_the_ring(block, axis, d):
+    size = lax.axis_size(axis)
+    hops = [(i, (i + 1) % size) for i in range(size)]
+    parts = [block]
+    for reach in range(1, size):
+        parts = [lax.ppermute(parts[0], axis, hops), *parts]
+    full = jnp.concatenate(parts, axis=d)
+    shift = (lax.axis_index(axis) + 1) * parts[-1].shape[d]
+    return jnp.roll(full, shift, axis=d)
 
 
 def squared_norms(rows_in):
@@ -73,7 +84,7 @@
     chosen_rows = jnp.take(flattened, block_owner * capacity + own_rank, axis=0)
     per_block = PANEL_DEV // col_count
     piece = lax.dynamic_slice_in_dim(chosen_rows, col_index * per_block, per_block, 0)
-    column_rows = lax.all_gather(piece, "rows", axis=0, tiled=True)
+    column_rows = around_the_ring(piece, "rows", 0)
     panel = kernel_values(chosen_rows, column_rows, squared_norms(column_rows), rate_value, depth)
     return (leverage, panel)
 

time: 144 us -> 145 us (level)
  blocking collectives: 30.3 us -> 17.1 us
  waiting for transfers between devices: 47.9 us -> 60.6 us
    ppermute x0 -> x3, waiting for transfers between devices: none -> 14.5 us  [around_the_ring(): parts = [lax.ppermute(parts[0], axis, hops), *parts]]
    all_gather x1 -> x0, blocking collectives: 13.2 us -> none  [shards(): column_rows = lax.all_gather(piece, 'rows', axis=0, tiled=True)]
    all_gather x1, waiting for transfers between devices: 36.9 us -> 33.9 us  [shards(): factor_cols = lax.all_gather(mixed, 'rows', axis=0, tiled=True)]
  transfers between devices with their start and end apart: 4 -> 7, of which waited for: 3 -> 6; matrix products, arithmetic and copies ran while one was open for 8% -> 8% of each run, Pallas kernels for 0% -> 0%
where the time goes in v1:
time: 145 us; the launch traced here: 144 us
  waiting for transfers between devices  60.6 us (42%)
  matrix products  27 us (19%)
  blocking collectives  17.1 us (12%)
  between operations  14.9 us (10%)
  starting transfers between devices  10.5 us (7%)
  other arithmetic  6.91 us (5%)
  local copies, waits for them, and re-layouts  6.85 us (5%)
    all_gather x1, waiting for transfers between devices, shards(): factor_cols = lax.all_gather(mixed, 'rows', axis=0, tiled=True)  33.9 us
    dot_general x8, matrix products, block_total(): projected = jnp.dot(values, factor_cols, preferred_element_type=jnp.float32)  26.1 us
    ppermute x3, waiting for transfers between devices, around_the_ring(): parts = [lax.ppermute(parts[0], axis, hops), *parts]  14.5 us
    all_gather x1, blocking collectives, shards(): arrived = lax.all_gather(moved, ('cols', 'sub'), axis=1, tiled=True)  9.58 us
    all_to_all x1, waiting for transfers between devices, shards(): lax.all_to_all(outgoing, 'rows', split_axis=0, concat_axis=0, tiled=True)  5.9 us
    all_to_all x1, waiting for transfers between devices, shards(): lax.all_to_all(factor, 'cols', split_axis=1, concat_axis=0, tiled=True)  5.61 us
    all_to_all x1, starting transfers between devices, shards(): lax.all_to_all(outgoing, 'rows', split_axis=0, concat_axis=0, tiled=True)  5.12 us
    unnamed x1, blocking collectives  5 us
  transfers between devices with their start and end apart: 7, of which 6 were waited for; matrix products, arithmetic and copies ran while one was open for 8% of the time, Pallas kernels for 0%

profile of v1, /device:TPU:0, one launch (start us, length us, event | category | flops | bytes accessed | tf_op | source)
XLA Modules:
  0.0 144.0 jit_solution(8793351542890969113)
XLA Ops:
  7.9 1.9 %copy.21 = bf16[32,2,8,512]{3,2,0,1:T(8,128)(2,1)} copy(bf16[32,2,8,512]{3,2,1,0:T(8,128)(2,1)} %bitcast.50) | data formatting | bytes 1048576 | tf_op jit(solution)/shard_map/all_to_all | solution.py:45
  9.8 4.2 %all-to-all-start = ((bf16[256,2,512]{2,0,1:T(8,128)(2,1)}), bf16[256,2,512]{2,0,1:T(8,128)(2,1)S(1)}, u32[]{:S(2)}, u32[]{:S(2)}) async-start(bf16[256,2,512]{2,0,1:T(8,128)(2,1)} %bitcast.36), calls=%async_computation | async-start | bytes 1048576 | tf_op jit(solution)/shard_map/all_to_all | solution.py:45
  15.2 1.2 reduce-window.6
  17.1 5.6 %all-to-all-done = bf16[256,2,512]{2,0,1:T(8,128)(2,1)S(1)} async-done(((bf16[256,2,512]{2,0,1:T(8,128)(2,1)}), bf16[256,2,512]{2,0,1:T(8,128)(2,1)S(1)}, u32[]{:S(2)}, u32[]{:S(2)}) %all-to-all-start) | async-done | bytes 524320 | tf_op jit(solution)/shard_map/all_to_all | solution.py:45
  23.9 1.2 gather_fusion
  26.1 5.1 %all-to-all-start.1 = ((bf16[4,64,256]{2,1,0:T(8,128)(2,1)}), bf16[4,64,256]{2,1,0:T(8,128)(2,1)S(1)}, u32[]{:S(2)}, u32[]{:S(2)}) async-start(bf16[4,64,256]{2,1,0:T(8,128)(2,1)} %select_select_fusion), calls=%async_computation.1 | async-start | bytes 262144 | tf_op jit(solution)/shard_map/all_to_all | solution.py:77
  31.2 5.9 %all-to-all-done.1 = bf16[4,64,256]{2,1,0:T(8,128)(2,1)S(1)} async-done(((bf16[4,64,256]{2,1,0:T(8,128)(2,1)}), bf16[4,64,256]{2,1,0:T(8,128)(2,1)S(1)}, u32[]{:S(2)}, u32[]{:S(2)}) %all-to-all-start.1) | async-done | bytes 131104 | tf_op jit(solution)/shard_map/all_to_all | solution.py:77
  37.1 9.6 %all_gather.11 = bf16[4,256,256]{2,1,0:T(8,128)(2,1)S(1)} all-gather(bf16[4,64,256]{2,1,0:T(8,128)(2,1)S(1)} %all-to-all-done.1), channel_id=1, replica_groups=mesh['groups'=2,'rows'=4,'cols'=2,'sub'=2] {'cols','sub'}, dimensions={1}, use_global_device_ids=true | all-gather | bytes 655360 | tf_op jit(solution)/shard_map/all_gather | solution.py:78
  49.2 4.7 %collective-permute-done = bf16[32,256]{1,0:T(8,128)(2,1)S(1)} collective-permute-done((bf16[32,256]{1,0:T(8,128)(2,1)S(1)}, bf16[32,256]{1,0:T(8,128)(2,1)S(1)}, u32[]{:S(2)}, u32[]{:S(2)}) %collective-permute-start) | collective-permute-done | bytes 16416 | tf_op jit(solution)/shard_map/ppermute | solution.py:15
  53.9 5.5 %collective-permute-done.1 = bf16[32,256]{1,0:T(8,128)(2,1)S(1)} collective-permute-done((bf16[32,256]{1,0:T(8,128)(2,1)S(1)}, bf16[32,256]{1,0:T(8,128)(2,1)S(1)}, u32[]{:S(2)}, u32[]{:S(2)}) %collective-permute-start.1) | collective-permute-done | bytes 16416 | tf_op jit(solution)/shard_map/ppermute | solution.py:15
  60.7 4.3 %collective-permute-done.2 = bf16[32,256]{1,0:T(8,128)(2,1)S(1)} collective-permute-done((bf16[32,256]{1,0:T(8,128)(2,1)S(1)}, bf16[32,256]{1,0:T(8,128)(2,1)S(1)}, u32[]{:S(2)}, u32[]{:S(2)}) %collective-permute-start.2) | collective-permute-done | bytes 16416 | tf_op jit(solution)/shard_map/ppermute | solution.py:15
  66.0 1.6 %multiply_reduce_fusion.1 = f32[2048]{0:T(1024)S(1)} fusion(bf16[2048,256]{1,0:T(8,128)(2,1)} %all-gather.3.cloned.1.call-done), kind=kLoop, calls=%fused_computation.17 | loop fusion | flops 1570816 | bytes 1056768 | tf_op jit(solution)/shard_map/reduce_sum | solution.py:22
  67.6 33.9 %all-gather.5.cloned.1.call-done = bf16[2048,512]{1,0:T(8,128)(2,1)} async-done(((bf16[512,512]{1,0:T(8,128)(2,1)}), bf16[2048,512]{1,0:T(8,128)(2,1)}) %all-gather.5.cloned.1.call-update) | async-done | bytes 2097168 | tf_op jit(solution)/shard_map/all_gather | solution.py:46
  101.5 27.6 %while.10 = (s32[]{:T(128)}, f32[8,256]{1,0:T(8,128)S(1)}, bf16[8,256,256]{2,1,0:T(8,128)(2,1)S(1)}, f32[2048]{0:T(1024)S(1)}, bf16[2048,256]{1,0:T(8,128)(2,1)}...) while((s32[]{:T(128)}, f32[8,256]{1,0:T(8,128)S(1)}, bf16[8,256,256]{2,1,0:T(8,128)(2,1)S(1)}, ...), condition=%wide.region_4.5_spmd, body=%wide.region_1.4_spmd.sunk | while | flops 808910336 | bytes 3421289 | solution.py:56
  101.6 3.3 %fusion.33 = f32[256]{0:T(256)S(1)} fusion(bf16[2048,512]{1,0:T(8,128)(2,1)} %get-tuple-element.111, bf16[2048,256]{1,0:T(8,128)(2,1)} %get-tuple-element.110, f32[2048]{0:T(1024)S(1)} %get-tuple-element.109, f32[256]{0:T(256)S(1)} %multiply_reduce_fusion.5, bf16[8,256,256]{2,1,0:T(8,128)(2,1)S(1)} %get-tuple-element.108, s32[]{:T(128)S(6)} %copy.25), kind=kOutput, calls=%fused_computation.9.clone.1 | convolution fusion | flops 808713984 | bytes 3287044 | tf_op jit(solution)/shard_map/while/body/eval_jaxpr/dot_general | solution.py:53
  105.1 3.3 %fusion.33 = f32[256]{0:T(256)S(1)} fusion(bf16[2048,512]{1,0:T(8,128)(2,1)} %get-tuple-element.111, bf16[2048,256]{1,0:T(8,128)(2,1)} %get-tuple-element.110, f32[2048]{0:T(1024)S(1)} %get-tuple-element.109, f32[256]{0:T(256)S(1)} %multiply_reduce_fusion.5, bf16[8,256,256]{2,1,0:T(8,128)(2,1)S(1)} %get-tuple-element.108, s32[]{:T(128)S(6)} %copy.25), kind=kOutput, calls=%fused_computation.9.clone.1 | convolution fusion | flops 808713984 | bytes 3287044 | tf_op jit(solution)/shard_map/while/body/eval_jaxpr/dot_general | solution.py:53
  108.5 3.3 %fusion.33 = f32[256]{0:T(256)S(1)} fusion(bf16[2048,512]{1,0:T(8,128)(2,1)} %get-tuple-element.111, bf16[2048,256]{1,0:T(8,128)(2,1)} %get-tuple-element.110, f32[2048]{0:T(1024)S(1)} %get-tuple-element.109, f32[256]{0:T(256)S(1)} %multiply_reduce_fusion.5, bf16[8,256,256]{2,1,0:T(8,128)(2,1)S(1)} %get-tuple-element.108, s32[]{:T(128)S(6)} %copy.25), kind=kOutput, calls=%fused_computation.9.clone.1 | convolution fusion | flops 808713984 | bytes 3287044 | tf_op jit(solution)/shard_map/while/body/eval_jaxpr/dot_general | solution.py:53
  112.0 3.3 %fusion.33 = f32[256]{0:T(256)S(1)} fusion(bf16[2048,512]{1,0:T(8,128)(2,1)} %get-tuple-element.111, bf16[2048,256]{1,0:T(8,128)(2,1)} %get-tuple-element.110, f32[2048]{0:T(1024)S(1)} %get-tuple-element.109, f32[256]{0:T(256)S(1)} %multiply_reduce_fusion.5, bf16[8,256,256]{2,1,0:T(8,128)(2,1)S(1)} %get-tuple-element.108, s32[]{:T(128)S(6)} %copy.25), kind=kOutput, calls=%fused_computation.9.clone.1 | convolution fusion | flops 808713984 | bytes 3287044 | tf_op jit(solution)/shard_map/while/body/eval_jaxpr/dot_general | solution.py:53
  115.4 3.3 %fusion.33 = f32[256]{0:T(256)S(1)} fusion(bf16[2048,512]{1,0:T(8,128)(2,1)} %get-tuple-element.111, bf16[2048,256]{1,0:T(8,128)(2,1)} %get-tuple-element.110, f32[2048]{0:T(1024)S(1)} %get-tuple-element.109, f32[256]{0:T(256)S(1)} %multiply_reduce_fusion.5, bf16[8,256,256]{2,1,0:T(8,128)(2,1)S(1)} %get-tuple-element.108, s32[]{:T(128)S(6)} %copy.25), kind=kOutput, calls=%fused_computation.9.clone.1 | convolution fusion | flops 808713984 | bytes 3287044 | tf_op jit(solution)/shard_map/while/body/eval_jaxpr/dot_general | solution.py:53
  118.9 3.3 %fusion.33 = f32[256]{0:T(256)S(1)} fusion(bf16[2048,512]{1,0:T(8,128)(2,1)} %get-tuple-element.111, bf16[2048,256]{1,0:T(8,128)(2,1)} %get-tuple-element.110, f32[2048]{0:T(1024)S(1)} %get-tuple-element.109, f32[256]{0:T(256)S(1)} %multiply_reduce_fusion.5, bf16[8,256,256]{2,1,0:T(8,128)(2,1)S(1)} %get-tuple-element.108, s32[]{:T(128)S(6)} %copy.25), kind=kOutput, calls=%fused_computation.9.clone.1 | convolution fusion | flops 808713984 | bytes 3287044 | tf_op jit(solution)/shard_map/while/body/eval_jaxpr/dot_general | solution.py:53
  122.3 3.3 %fusion.33 = f32[256]{0:T(256)S(1)} fusion(bf16[2048,512]{1,0:T(8,128)(2,1)} %get-tuple-element.111, bf16[2048,256]{1,0:T(8,128)(2,1)} %get-tuple-element.110, f32[2048]{0:T(1024)S(1)} %get-tuple-element.109, f32[256]{0:T(256)S(1)} %multiply_reduce_fusion.5, bf16[8,256,256]{2,1,0:T(8,128)(2,1)S(1)} %get-tuple-element.108, s32[]{:T(128)S(6)} %copy.25), kind=kOutput, calls=%fused_computation.9.clone.1 | convolution fusion | flops 808713984 | bytes 3287044 | tf_op jit(solution)/shard_map/while/body/eval_jaxpr/dot_general | solution.py:53
  125.8 3.3 %fusion.33 = f32[256]{0:T(256)S(1)} fusion(bf16[2048,512]{1,0:T(8,128)(2,1)} %get-tuple-element.111, bf16[2048,256]{1,0:T(8,128)(2,1)} %get-tuple-element.110, f32[2048]{0:T(1024)S(1)} %get-tuple-element.109, f32[256]{0:T(256)S(1)} %multiply_reduce_fusion.5, bf16[8,256,256]{2,1,0:T(8,128)(2,1)S(1)} %get-tuple-element.108, s32[]{:T(128)S(6)} %copy.25), kind=kOutput, calls=%fused_computation.9.clone.1 | convolution fusion | flops 808713984 | bytes 3287044 | tf_op jit(solution)/shard_map/while/body/eval_jaxpr/dot_general | solution.py:53
  129.1 5.0 %all-reduce = f32[2048]{0:T(1024)S(1)} all-reduce(f32[2048]{0:T(1024)S(1)} %bitcast.52), channel_id=2, replica_groups=mesh['groups'=2,'rows'=4,'cols'=2,'sub'=2] {'cols'}, use_global_device_ids=true, to_apply=%region_5.6.clone | all-reduce | flops 2048 | bytes 16384
  134.1 2.5 %psum.7 = f32[1024]{0:T(1024)S(1)} all-reduce(f32[1024]{0:T(1024)S(1)} %dynamic-slice.1), channel_id=1, replica_groups=mesh['groups'=2,'rows'=4,'cols'=2,'sub'=2] {'sub'}, use_global_device_ids=true, to_apply=%region_6.7 | all-reduce | flops 1024 | bytes 8192 | tf_op jit(solution)/shard_map/psum | solution.py:58
  (78 shorter events, 10.7 us)
Async XLA Ops:
  7.2 7.4 %copy-start.2 = (s32[1024,1]{0,1:T(1,128)S(1)}, s32[1024,1]{0,1:T(1,128)}, u32[]{:S(2)}) copy-start(s32[1024,1]{0,1:T(1,128)} %param.10) | copy-start | bytes 12292
  7.2 9.7 %copy-start.3 = (s32[1024]{0:T(1024)S(1)}, s32[1024]{0:T(1024)}, u32[]{:S(2)}) copy-start(s32[1024]{0:T(1024)} %param.11) | copy-start | bytes 12292
  7.2 16.7 %copy-start = (bf16[2048,256]{1,0:T(8,128)(2,1)S(1)}, bf16[2048,256]{1,0:T(8,128)(2,1)}, u32[]{:S(2)}) copy-start(bf16[2048,256]{1,0:T(8,128)(2,1)} %param.7) | copy-start | bytes 3145732
  7.2 58.8 %all-gather.3.cloned.1.call-start = ((), (), s32[]{:S(2)}) async-start(), calls=%async_computation.2 | async-start | bytes 1179648 | tf_op jit(solution)/shard_map/all_gather | solution.py:44
  9.8 13.0 %all-to-all-start = ((bf16[256,2,512]{2,0,1:T(8,128)(2,1)}), bf16[256,2,512]{2,0,1:T(8,128)(2,1)S(1)}, u32[]{:S(2)}, u32[]{:S(2)}) async-start(bf16[256,2,512]{2,0,1:T(8,128)(2,1)} %bitcast.36), calls=%async_computation | async-start | bytes 1048576 | tf_op jit(solution)/shard_map/all_to_all | solution.py:45
  14.0 87.5 %all-gather.5.cloned.1.call-start = ((), (), s32[]{:S(2)}) async-start(), calls=%async_computation.3 | async-start | bytes 2621440 | tf_op jit(solution)/shard_map/all_gather | solution.py:46
  22.8 0.8 copy-start.1
  23.6 35.9 %copy-start.4 = (u32[32]{0:T(128)S(1)}, u32[32]{0:T(128)}, u32[]{:S(2)}) copy-start(u32[32]{0:T(128)} %constant.126) | copy-start | bytes 388
  26.1 11.0 %all-to-all-start.1 = ((bf16[4,64,256]{2,1,0:T(8,128)(2,1)}), bf16[4,64,256]{2,1,0:T(8,128)(2,1)S(1)}, u32[]{:S(2)}, u32[]{:S(2)}) async-start(bf16[4,64,256]{2,1,0:T(8,128)(2,1)} %select_select_fusion), calls=%async_computation.1 | async-start | bytes 262144 | tf_op jit(solution)/shard_map/all_to_all | solution.py:77
  48.1 5.8 %collective-permute-start = (bf16[32,256]{1,0:T(8,128)(2,1)S(1)}, bf16[32,256]{1,0:T(8,128)(2,1)S(1)}, u32[]{:S(2)}, u32[]{:S(2)}) collective-permute-start(bf16[32,256]{1,0:T(8,128)(2,1)S(1)} %constant_dynamic-slice_fusion), channel_id=1, source_target_pairs={{0,4},{4,8},{8,12},{12,0},{1,5},{5,9},{9,13},{13,1},{2,6},{6,10},{... | collective-permute-start | bytes 49160 | tf_op jit(solution)/shard_map/ppermute | solution.py:15
  53.9 5.5 %collective-permute-start.1 = (bf16[32,256]{1,0:T(8,128)(2,1)S(1)}, bf16[32,256]{1,0:T(8,128)(2,1)S(1)}, u32[]{:S(2)}, u32[]{:S(2)}) collective-permute-start(bf16[32,256]{1,0:T(8,128)(2,1)S(1)} %collective-permute-done), channel_id=1, source_target_pairs={{0,4},{4,8},{8,12},{12,0},{1,5},{5,9},{9,13},{13,1},{2,6},{6,10},{... | collective-permute-start | bytes 49160 | tf_op jit(solution)/shard_map/ppermute | solution.py:15
  59.4 5.5 %collective-permute-start.2 = (bf16[32,256]{1,0:T(8,128)(2,1)S(1)}, bf16[32,256]{1,0:T(8,128)(2,1)S(1)}, u32[]{:S(2)}, u32[]{:S(2)}) collective-permute-start(bf16[32,256]{1,0:T(8,128)(2,1)S(1)} %collective-permute-done.1), channel_id=1, source_target_pairs={{0,4},{4,8},{8,12},{12,0},{1,5},{5,9},{9,13},{13,1},{2,6},{6,10},{... | collective-permute-start | bytes 49160 | tf_op jit(solution)/shard_map/ppermute | solution.py:15
Sparse Core Ops, SparseCore 0:
  10.1 43.8 all-gather.2
  55.6 45.8 all-gather.4
